TPU v7x, 32 devices: a whole 2x2x4 slice. The times are simulated.
32 devices in a mesh: groups: 2 (over y), expert: 16 (over z, x, core), head: 1.
Axes of the slice: x: 2, y: 2, z: 4, core: 2. Of those that a mesh axis runs over, the one named last changes fastest.
Arguments:
- sources: bfloat16 [4096, 1024], P(('groups', 'expert')), parts along dimension 0, may hold values from -6 to 6
- enc_gain: float32 [1024], replicated, may hold values from 0.1 to 1.9
- route_ids: int32 [4096, 2], P(('groups', 'expert')), parts along dimension 0, may hold values from 0 to 7, all different within a row; in each aligned block of 128 rows (0 to 127, 128 to 255, ...) at most 40 rows name the same one
- route_gates: float32 [4096, 2], P(('groups', 'expert')), parts along dimension 0, may hold values from 0.2 to 1
- w_in: bfloat16 [16, 1024, 2048], P('expert', None, 'head'), may hold values from -0.1875 to 0.1875
- w_out: bfloat16 [16, 2048, 1024], P('expert', 'head'), may hold values from -0.09375 to 0.09375
- targets: bfloat16 [4096, 1024], P(('groups', 'expert')), parts along dimension 0, may hold values from -6 to 6
- dec_gain: float32 [1024], replicated, may hold values from 0.1 to 1.9
- src_lengths: int32 [64], P(('groups', 'expert')), parts along dimension 0, may hold values from 16 to 64, as said below
- tgt_lengths: int32 [64], P(('groups', 'expert')), parts along dimension 0, may hold values from 16 to 64, as said below
- w_query: bfloat16 [1024, 1024], P('expert', 'head'), may hold values from -60 to 60
- w_key: bfloat16 [1024, 1024], P('expert', 'head'), may hold values from -0.1875 to 0.1875
- w_value: bfloat16 [1024, 1024], P('expert', 'head'), may hold values from -0.1875 to 0.1875
- w_attn: bfloat16 [1024, 1024], P('expert', 'head'), may hold values from -0.1875 to 0.1875
Outputs:
- memory: bfloat16 [4096, 1024], P(('groups', 'expert')), parts along dimension 0
- decoded: bfloat16 [4096, 1024], P(('groups', 'expert'), 'head'), parts along dimension 0
There are 2 independent parts, one for each index of `groups`. A program takes and returns all parts, laid end to end along the dimension named above; an argument that names none is the same for every part. Nothing has to cross between parts.
Inputs may be any that keep to these rules, and one draw needn't show every extreme that they name: `route_ids`: in each aligned block of 128 rows no expert is named more than 40 times, a bound that some block reaches. `src_lengths`: some sentence has exactly 64 live tokens. `tgt_lengths`: some sentence has exactly 64 live tokens.
All inputs are finite; a program needn't handle non-finite values.
Results may differ from a plain program's by a relative error of at most 0.025.
Values may be sent and summed in bfloat16 or wider, within the bound.
A program may use at most 64 MiB of HBM per device.

v0:
```python
import jax
import jax.numpy as jnp
from jax import lax
from jax.sharding import PartitionSpec as P

DH = 64


def from_partner(x, axis, stride):
    return lax.ppermute(x, axis, [(i, i ^ 1 << stride) for i in range(lax.axis_size(axis))])


def layer_norm(rows, gain):
    rows = rows.astype(jnp.float32)
    mean = jnp.mean(rows, axis=-1, keepdims=True)
    centered = rows - mean
    spread = jnp.mean(centered * centered, axis=-1, keepdims=True)
    return centered * lax.rsqrt(spread + 1e-05) * gain


def partner(block):
    return from_partner(block, "expert", 0)


def shards(
    sources,
    enc_gain,
    route_ids,
    route_gates,
    w_in,
    w_out,
    targets,
    dec_gain,
    src_lengths,
    tgt_lengths,
    w_query,
    w_key,
    w_value,
    w_attn,
):
    tok_rows, width = sources.shape
    experts = lax.axis_size("expert") // 2
    capacity = 2 * ((5 * tok_rows + 4 * experts - 1) // (4 * experts))
    side = lax.axis_index("expert") % 2
    pair_ids = route_ids.reshape(-1)
    onehot = (pair_ids[:, None] == jnp.arange(experts, dtype=jnp.int32)[None, :]).astype(jnp.int32)
    earlier = jnp.cumsum(onehot, axis=0) - onehot
    slots = jnp.sum(earlier * onehot, axis=1)
    place = pair_ids * capacity + slots
    normed = layer_norm(sources, enc_gain).astype(jnp.bfloat16)
    outgoing = (
        jnp.zeros((experts * capacity, width), jnp.bfloat16)
        .at[place]
        .set(jnp.repeat(normed, 2, axis=0))
    )
    sending = outgoing.reshape(2 * experts, capacity // 2, width)
    arrived = lax.all_to_all(sending, "expert", split_axis=0, concat_axis=0, tiled=True)
    other = partner(arrived)
    lower = jnp.where(side == 0, arrived, other)
    upper = jnp.where(side == 0, other, arrived)
    arrived = jnp.concatenate((lower, upper), axis=1)
    expert_rows = arrived.reshape(-1, width)
    hidden = jnp.maximum(
        jnp.dot(expert_rows, w_in[0], preferred_element_type=jnp.float32), 0.0
    ).astype(jnp.bfloat16)
    quarter = jnp.dot(hidden, w_out[0], preferred_element_type=jnp.float32)
    half = lax.psum(quarter.astype(jnp.bfloat16), "head")
    kept = half.shape[1]
    half = half.reshape(2 * experts, capacity, kept)
    other_half = partner(half)
    merged = (half.astype(jnp.float32) + other_half.astype(jnp.float32)).astype(jnp.bfloat16)
    leaving = lax.dynamic_slice_in_dim(merged, side * (capacity // 2), capacity // 2, 1)
    returned = lax.all_to_all(leaving, "expert", split_axis=0, concat_axis=0, tiled=True)
    results = returned.reshape(-1, kept)
    picked = jnp.take(results, place, axis=0).astype(jnp.float32).reshape(tok_rows, 2, kept)
    moe = route_gates[:, 0:1] * picked[:, 0, :] + route_gates[:, 1:2] * picked[:, 1, :]
    memory = (sources.astype(jnp.float32) + moe).astype(jnp.bfloat16)
    w_q, w_k, w_v, w_o = (
        lax.all_gather(w_query, "expert", axis=0, tiled=True),
        lax.all_gather(w_key, "expert", axis=0, tiled=True),
        lax.all_gather(w_value, "expert", axis=0, tiled=True),
        lax.all_gather(w_attn, "expert", axis=0, tiled=True),
    )
    tnormed = layer_norm(targets, dec_gain).astype(jnp.bfloat16)
    query = jnp.dot(tnormed, w_q, preferred_element_type=jnp.float32).astype(jnp.bfloat16)
    key = jnp.dot(memory, w_k, preferred_element_type=jnp.float32).astype(jnp.bfloat16)
    value = jnp.dot(memory, w_v, preferred_element_type=jnp.float32).astype(jnp.bfloat16)
    sentences = src_lengths.shape[0]
    local_heads = query.shape[1] // DH
    queries = query.reshape(sentences, -1, local_heads, DH)
    keys = key.reshape(sentences, -1, local_heads, DH)
    values = value.reshape(sentences, -1, local_heads, DH)
    key_count = keys.shape[1]
    scores = jnp.einsum(
        "sqhd,skhd->shqk", queries, keys, preferred_element_type=jnp.float32
    ) * DH ** (-0.5)
    live = jnp.arange(key_count, dtype=jnp.int32)[None, :] < src_lengths[:, None]
    scores = jnp.where(live[:, None, None, :], scores, -1e30)
    top = jnp.max(scores, axis=-1, keepdims=True)
    raised = jnp.exp(scores - top)
    weights = (raised / jnp.sum(raised, axis=-1, keepdims=True)).astype(jnp.bfloat16)
    context = jnp.einsum(
        "shqk,skhd->sqhd", weights, values, preferred_element_type=jnp.float32
    ).astype(jnp.bfloat16)
    context = context.reshape(targets.shape[0], -1)
    partial_out = lax.dot_general(
        context, w_o, (((1,), (1,)), ((), ())), preferred_element_type=jnp.float32
    )
    attn = lax.psum_scatter(
        partial_out.astype(jnp.bfloat16), "head", scatter_dimension=1, tiled=True
    ).astype(jnp.float32)
    share = width // lax.axis_size("head")
    own_targets = lax.dynamic_slice_in_dim(
        targets, lax.axis_index("head") * share, share, 1
    ).astype(jnp.float32)
    per_sentence = targets.shape[0] // sentences
    positions = jnp.arange(targets.shape[0], dtype=jnp.int32)
    owner = positions // per_sentence
    live_rows = (positions % per_sentence < jnp.take(tgt_lengths, owner)).astype(jnp.float32)
    decoded = ((own_targets + attn) * live_rows[:, None]).astype(jnp.bfloat16)
    return (memory, decoded)


def solution(mesh):
    placed = (
        P(("groups", "expert"), None),
        P(),
        P(("groups", "expert"), None),
        P(("groups", "expert"), None),
        P("expert", None, "head"),
        P("expert", "head", None),
        P(("groups", "expert"), None),
        P(),
        P(("groups", "expert")),
        P(("groups", "expert")),
        P("expert", "head"),
        P("expert", "head"),
        P("expert", "head"),
        P("expert", "head"),
    )
    return jax.shard_map(
        shards,
        mesh=mesh,
        in_specs=placed,
        out_specs=(P(("groups", "expert"), None), P(("groups", "expert"), "head")),
        check_vma=False,
    )
```

profile of v0, /device:TPU:0, one launch (start us, length us, event | category | flops | bytes accessed | tf_op | source)
XLA Modules:
  0.0 201.5 jit_solution(6229918482698029241)
XLA Ops:
  7.2 0.7 all-gather.7.cloned.1.call-update
  7.9 0.7 all-gather.5.cloned.1.call-update
  8.6 0.8 copy.44
  9.7 0.7 broadcast_multiply_fusion
  10.7 0.6 reduce-window.6
  11.3 0.2 slice_reduce_fusion
  11.5 1.1 convert_reduce_fusion.1
  12.6 1.2 fusion.27
  13.8 1.2 fusion.29
  15.0 0.3 broadcast_in_dim.50
  15.2 0.2 reshape.235
  15.5 1.9 scatter_custom_fusion
  17.4 1.0 reshape.206
  18.5 7.4 %all-to-all-start = ((bf16[16,20,1024]{2,1,0:T(8,128)(2,1)}), bf16[16,20,1024]{2,1,0:T(8,128)(2,1)S(1)}, u32[]{:S(2)}, u32[]{:S(2)}) async-start(bf16[16,20,1024]{2,1,0:T(8,128)(2,1)} %reshape.206), calls=%async_computation | async-start | bytes 1572864 | tf_op jit(solution)/shard_map/all_to_all | solution.py:57
  25.9 0.7 all-gather.9.cloned.1.call-update
  26.6 18.8 %all-to-all-done = bf16[16,20,1024]{2,1,0:T(8,128)(2,1)S(1)} async-done(((bf16[16,20,1024]{2,1,0:T(8,128)(2,1)}), bf16[16,20,1024]{2,1,0:T(8,128)(2,1)S(1)}, u32[]{:S(2)}, u32[]{:S(2)}) %all-to-all-start) | async-done | bytes 655392 | tf_op jit(solution)/shard_map/all_to_all | solution.py:57
  45.5 0.4 copy.48
  45.8 0.4 collective-permute-start
  46.3 1.8 collective-permute-done
  48.1 0.4 broadcast_select_fusion.1
  48.5 0.3 pad_maximum_fusion
  48.8 9.1 %fusion.7 = bf16[640,1024]{1,0:T(8,128)(2,1)S(1)} fusion(bf16[1,2048,1024]{2,1,0:T(8,128)(2,1)} %param.19, bf16[640,1024]{1,0:T(8,128)(2,1)S(1)} %bitcast.61, bf16[1,1024,2048]{2,1,0:T(8,128)(2,1)} %param.18), kind=kOutput, calls=%fused_computation.8 | convolution fusion | flops 5371985920 | bytes 11010048 | tf_op jit(solution)/shard_map/dot_general | solution.py:66
  57.9 0.4 collective-permute-start.1
  58.4 0.6 fusion.55
  59.1 0.2 fusion.24
  59.4 1.7 collective-permute-done.1
  61.1 1.5 add_convert_fusion
  62.6 11.8 %all-to-all-start.1 = ((bf16[16,20,1024]{2,1,0:T(8,128)(2,1)}), bf16[16,20,1024]{2,1,0:T(8,128)(2,1)S(1)}, u32[]{:S(2)}, u32[]{:S(2)}) async-start(bf16[16,20,1024]{2,1,0:T(8,128)(2,1)} %add_convert_fusion), calls=%async_computation.1 | async-start | bytes 1572864 | tf_op jit(solution)/shard_map/all_to_all | solution.py:73
  74.4 1.3 compare_convert_fusion
  76.1 2.1 %convolution_convert_fusion.3 = bf16[128,1024]{1,0:T(8,128)(2,1)S(1)} fusion(bf16[1024,1024]{1,0:T(8,128)(2,1)} %all-gather.7.cloned.1.call-done, bf16[128,1024]{1,0:T(8,128)(2,1)S(1)} %copy-done, f32[1024]{0:T(1024)S(1)} %copy-done.4, f32[128]{0:T(128)S(1)} %add_rsqrt_fusion, f32[128]{0:T(128)S(1)} %broadcast_multiply_fusion.1), kind=kOutput, calls=%fused_computation.23 | convolution fusion | flops 269221888 | bytes 2626560 | tf_op jit(solution)/shard_map/dot_general | solution.py:85
  78.2 0.3 reshape.211
  78.5 15.2 %all-to-all-done.1 = bf16[16,20,1024]{2,1,0:T(8,128)(2,1)S(1)} async-done(((bf16[16,20,1024]{2,1,0:T(8,128)(2,1)}), bf16[16,20,1024]{2,1,0:T(8,128)(2,1)S(1)}, u32[]{:S(2)}, u32[]{:S(2)}) %all-to-all-start.1) | async-done | bytes 655392 | tf_op jit(solution)/shard_map/all_to_all | solution.py:73
  93.8 1.2 gather_fusion
  95.2 0.2 fusion.37
  95.4 0.5 copy-done.1
  96.1 11.1 %all-gather.5.cloned.1.call-done = bf16[1024,1024]{1,0:T(8,128)(2,1)} async-done(((bf16[64,1024]{1,0:T(8,128)(2,1)}), bf16[1024,1024]{1,0:T(8,128)(2,1)}) %all-gather.5.cloned.1.call-update) | async-done | bytes 2097168 | tf_op jit(solution)/shard_map/all_gather | solution.py:81
  107.2 2.0 %convolution_convert_fusion.4 = bf16[128,1024]{1,0:T(8,128)(2,1)S(1)} fusion(bf16[128,1024]{1,0:T(8,128)(2,1)S(1)} %fusion.30, bf16[1024,1024]{1,0:T(8,128)(2,1)} %all-gather.5.cloned.1.call-done), kind=kOutput, calls=%fused_computation.24 | convolution fusion | flops 268566528 | bytes 2621440 | tf_op jit(solution)/shard_map/dot_general | solution.py:87
  109.3 0.3 reshape.210
  109.6 40.0 %all-gather.9.cloned.1.call-done = bf16[1024,1024]{1,0:T(8,128)(2,1)} async-done(((bf16[64,1024]{1,0:T(8,128)(2,1)}), bf16[1024,1024]{1,0:T(8,128)(2,1)}) %all-gather.9.cloned.1.call-update) | async-done | bytes 2097168 | tf_op jit(solution)/shard_map/all_gather | solution.py:80
  149.6 2.0 %convolution_convert_fusion.2 = bf16[128,1024]{1,0:T(8,128)(2,1)S(1)} fusion(bf16[128,1024]{1,0:T(8,128)(2,1)S(1)} %fusion.30, bf16[1024,1024]{1,0:T(8,128)(2,1)} %all-gather.9.cloned.1.call-done), kind=kOutput, calls=%fused_computation.22 | convolution fusion | flops 268566528 | bytes 2621440 | tf_op jit(solution)/shard_map/dot_general | solution.py:86
  151.7 0.3 reshape.212
  152.0 0.6 fusion.56
  152.6 1.4 fusion.12
  154.0 2.0 %fusion.13 = bf16[2,64,16,64]{1,3,2,0:T(8,128)(2,1)S(1)} fusion(bf16[2,64,16,64]{3,2,1,0:T(8,128)(2,1)S(1)} %reshape.210, f32[2,16,64]{2,1,0:T(8,128)S(1)} %fusion.56, f32[2,16,64,64]{2,3,1,0:T(8,128)} %fusion.12), kind=kOutput, calls=%fused_computation.16 | convolution fusion | flops 17303616 | bytes 1056768 | tf_op jit(solution)/shard_map/shqk,skhd->sqhd/dot_general | solution.py:102
  156.0 0.4 copy.56
  156.5 0.3 reshape.213
  156.8 35.0 %all-gather.11.cloned.1.call-done = bf16[1024,1024]{1,0:T(8,128)(2,1)} async-done(((bf16[64,1024]{1,0:T(8,128)(2,1)}), bf16[1024,1024]{1,0:T(8,128)(2,1)}) %all-gather.11.cloned.1.call-update) | async-done | bytes 2097168 | tf_op jit(solution)/shard_map/all_gather | solution.py:82
  191.8 3.1 %fusion.17 = bf16[128,1024]{1,0:T(8,128)(2,1)} fusion(bf16[128,1024]{1,0:T(8,128)(2,1)S(1)} %reshape.213, bf16[1024,1024]{1,0:T(8,128)(2,1)} %all-gather.11.cloned.1.call-done, bf16[128,1024]{1,0:T(8,128)(2,1)S(1)} %copy-done, f32[128]{0:T(128)S(1)} %compare_convert_fusion), kind=kOutput, calls=%fused_computation.21 | convolution fusion | flops 269221888 | bytes 2884096 | tf_op jit(solution)/shard_map/dot_general | solution.py:106
  (44 shorter events, 1.8 us)
Async XLA Ops:
  7.2 68.9 %all-gather.7.cloned.1.call-start = ((), (), s32[]{:S(2)}) async-start(), calls=%async_computation.3 | async-start | bytes 2228224 | tf_op jit(solution)/shard_map/all_gather | solution.py:79
  7.9 99.4 %all-gather.5.cloned.1.call-start = ((), (), s32[]{:S(2)}) async-start(), calls=%async_computation.2 | async-start | bytes 2228224 | tf_op jit(solution)/shard_map/all_gather | solution.py:81
  18.5 27.0 %all-to-all-start = ((bf16[16,20,1024]{2,1,0:T(8,128)(2,1)}), bf16[16,20,1024]{2,1,0:T(8,128)(2,1)S(1)}, u32[]{:S(2)}, u32[]{:S(2)}) async-start(bf16[16,20,1024]{2,1,0:T(8,128)(2,1)} %reshape.206), calls=%async_computation | async-start | bytes 1572864 | tf_op jit(solution)/shard_map/all_to_all | solution.py:57
  25.8 123.8 %all-gather.9.cloned.1.call-start = ((), (), s32[]{:S(2)}) async-start(), calls=%async_computation.4 | async-start | bytes 2228224 | tf_op jit(solution)/shard_map/all_gather | solution.py:80
  26.6 165.2 %all-gather.11.cloned.1.call-start = ((), (), s32[]{:S(2)}) async-start(), calls=%async_computation.5 | async-start | bytes 2228224 | tf_op jit(solution)/shard_map/all_gather | solution.py:82
  45.8 2.2 %collective-permute-start = (bf16[16,20,1024]{2,0,1:T(8,128)(2,1)S(1)}, bf16[16,20,1024]{2,0,1:T(8,128)(2,1)S(1)}, u32[]{:S(2)}, u32[]{:S(2)}) collective-permute-start(bf16[16,20,1024]{2,0,1:T(8,128)(2,1)S(1)} %copy.48), channel_id=1, source_target_pairs={{0,1},{1,0},{2,3},{3,2},{4,5},{5,4},{6,7},{7,6},{8,9},{9,8},{10,11... | collective-permute-start | bytes 1966088 | tf_op jit(solution)/shard_map/ppermute | solution.py:10
  48.8 9.6 %copy-start.5 = (s32[2]{0:T(128)S(1)}, s32[2]{0:T(128)}, u32[]{:S(2)}) copy-start(s32[2]{0:T(128)} %param.23) | copy-start | bytes 28
  48.8 10.2 %copy-start = (bf16[128,1024]{1,0:T(8,128)(2,1)S(1)}, bf16[128,1024]{1,0:T(8,128)(2,1)}, u32[]{:S(2)}) copy-start(bf16[128,1024]{1,0:T(8,128)(2,1)} %param.20) | copy-start | bytes 786436
  57.9 3.2 %collective-permute-start.1 = (bf16[16,40,1024]{2,1,0:T(8,128)(2,1)S(1)}, bf16[16,40,1024]{2,1,0:T(8,128)(2,1)S(1)}, u32[]{:S(2)}, u32[]{:S(2)}) collective-permute-start(bf16[16,40,1024]{2,1,0:T(8,128)(2,1)S(1)} %bitcast.62), channel_id=1, source_target_pairs={{0,1},{1,0},{2,3},{3,2},{4,5},{5,4},{6,7},{7,6},{8,9},{9,8},{10,11... | collective-permute-start | bytes 3932168 | tf_op jit(solution)/shard_map/ppermute | solution.py:10
  59.3 16.6 %copy-start.7 = (s32[2]{0:T(128)S(1)}, s32[2]{0:T(128)}, u32[]{:S(2)}) copy-start(s32[2]{0:T(128)} %param.22) | copy-start | bytes 28
  59.4 16.6 %copy-start.6 = (f32[128,2]{0,1:T(2,128)S(1)}, f32[128,2]{0,1:T(2,128)}, u32[]{:S(2)}) copy-start(f32[128,2]{0,1:T(2,128)} %param.17) | copy-start | bytes 3076
  59.4 16.6 %copy-start.3 = (s32[128,2]{0,1:T(2,128)S(1)}, s32[128,2]{0,1:T(2,128)}, u32[]{:S(2)}) copy-start(s32[128,2]{0,1:T(2,128)} %param.16) | copy-start | bytes 3076
  59.4 16.7 %copy-start.4 = (f32[1024]{0:T(1024)S(1)}, f32[1024]{0:T(1024)}, u32[]{:S(2)}) copy-start(f32[1024]{0:T(1024)} %param.21) | copy-start | bytes 12292
  62.6 31.1 %all-to-all-start.1 = ((bf16[16,20,1024]{2,1,0:T(8,128)(2,1)}), bf16[16,20,1024]{2,1,0:T(8,128)(2,1)S(1)}, u32[]{:S(2)}, u32[]{:S(2)}) async-start(bf16[16,20,1024]{2,1,0:T(8,128)(2,1)} %add_convert_fusion), calls=%async_computation.1 | async-start | bytes 1572864 | tf_op jit(solution)/shard_map/all_to_all | solution.py:73
  95.0 1.0 copy-start.1
  96.1 55.6 %copy-start.2 = (bf16[128,1024]{1,0:T(8,128)(2,1)}, bf16[128,1024]{1,0:T(8,128)(2,1)S(1)}, u32[]{:S(2)}) copy-start(bf16[128,1024]{1,0:T(8,128)(2,1)S(1)} %fusion.30) | copy-start | bytes 786436
Sparse Core Ops, SparseCore 0:
  10.1 49.4 all-gather.6
  61.8 45.4 all-gather.4
  109.4 40.1 all-gather.8
  151.6 40.1 all-gather.10
where the time goes:
time: 202 us; the launch traced here: 201 us
  waiting for transfers between devices  126 us (62%)
  matrix products  22.4 us (11%)
  starting transfers between devices  20.2 us (10%)
  between operations  14.1 us (7%)
  local copies, waits for them, and re-layouts  9.91 us (5%)
  other arithmetic  9.17 us (5%)
    all_gather x1, waiting for transfers between devices, shards(): lax.all_gather(w_key, 'expert', axis=0, tiled=True)  40 us
    all_gather x1, waiting for transfers between devices, shards(): lax.all_gather(w_attn, 'expert', axis=0, tiled=True)  35 us
    all_to_all x1, waiting for transfers between devices, shards(): lax.all_to_all(sending, 'expert', split_axis=0, concat_axis=0, tiled=True)  18.8 us
    all_to_all x1, waiting for transfers between devices, shards(): lax.all_to_all(leaving, 'expert', split_axis=0, concat_axis=0, tiled=True)  15.2 us
    all_to_all x1, starting transfers between devices, shards(): lax.all_to_all(leaving, 'expert', split_axis=0, concat_axis=0, tiled=True)  11.8 us
    all_gather x1, waiting for transfers between devices, shards(): lax.all_gather(w_value, 'expert', axis=0, tiled=True)  11.1 us
    dot_general x1, matrix products, shards(): quarter = jnp.dot(hidden, w_out[0], preferred_element_type=jnp.float32)  9.11 us
    all_to_all x1, starting transfers between devices, shards(): lax.all_to_all(sending, 'expert', split_axis=0, concat_axis=0, tiled=True)  7.39 us
  transfers between devices with their start and end apart: 8, of which 7 were waited for; matrix products, arithmetic and copies ran while one was open for 19% of the time, Pallas kernels for 0%

commit v1 on v0

--- a/solution.py
+++ b/solution.py
@@ -1,6 +1,8 @@
 import jax
 import jax.numpy as jnp
 from jax import lax
+from jax.experimental import pallas as pl
+from jax.experimental.pallas import tpu as pltpu
 from jax.sharding import PartitionSpec as P
 
 DH = 64
@@ -121,6 +123,412 @@
     return (memory, decoded)
 
 
+def fused_kernel(
+    src_len, tgt_len, sources, enc_gain, ids, gates, w_in, w_out, targets, dec_gain,
+    w_q, w_k, w_v, w_o, memory, decoded,
+    win, wout, wb, send, rows, hid, away, inbox, own, merged, back, tn, mem, bias, qkv, ctx, give, take,
+    loc_sem, pair_send, pair_recv, d_send, d_recv, c_send, c_recv,
+    w_recv, y_recv, up_send, dn_send, x_send, y_send,
+):
+    f32, bf16 = jnp.float32, jnp.bfloat16
+    peers = lax.axis_size("expert")
+    groups = lax.axis_size("groups")
+    me, g = lax.axis_index("expert"), lax.axis_index("groups")
+    p, chip = lax.rem(me, 2), lax.div(me, 2)
+    mate = chip * 2 + 1 - p
+    chips = peers // 2
+    nx = 2 if chips % 2 == 0 else 1
+    nz = chips // nx
+    x, z = lax.rem(chip, nx), lax.div(chip, nx)
+    tok, width = sources.shape
+    half = width // 2
+    cap = send.shape[1] // chips
+    shard = w_q.shape[0]
+    split = 2 if groups == 2 else 1
+    mats = 4 // split
+
+    def remote(src, dst, ss, rs, dev):
+        return pltpu.make_async_remote_copy(
+            src_ref=src, dst_ref=dst, send_sem=ss, recv_sem=rs,
+            device_id=dev, device_id_type=pl.DeviceIdType.MESH,
+        )
+
+    def dev_of(zz, xx):
+        return {"expert": (zz * nx + xx) * 2 + p}
+
+    weights = (w_q, w_k, w_v, w_o)
+    in_copy = pltpu.make_async_copy(w_in.at[0], win, loc_sem.at[0])
+    out_copy = pltpu.make_async_copy(w_out.at[0], wout, loc_sem.at[1])
+    own_rows = pl.ds(pl.multiple_of(me * shard, 16), shard)
+    w_copies = [
+        pltpu.make_async_copy(
+            w.at[:, pl.ds(pl.multiple_of(p * half, 128), half)], wb.at[i, own_rows, :], loc_sem.at[2 + i]
+        )
+        for i, w in enumerate(weights)
+    ]
+    for c in w_copies:
+        c.start()
+    in_copy.start()
+    out_copy.start()
+
+    barrier = pltpu.get_barrier_semaphore()
+    for d in range(1, peers):
+        pl.semaphore_signal(
+            barrier, inc=1, device_id={"expert": lax.rem(me + d, peers)},
+            device_id_type=pl.DeviceIdType.MESH,
+        )
+    if split == 2:
+        pl.semaphore_signal(
+            barrier, inc=1, device_id={"groups": 1 - g}, device_id_type=pl.DeviceIdType.MESH
+        )
+
+    eye = lax.broadcasted_iota(jnp.int32, (tok, chips), 1)
+    first = ids[:, 0:1]
+    second = ids[:, 1:2]
+    one0 = (eye == first).astype(f32)
+    one1 = (eye == second).astype(f32)
+    lower = (
+        lax.broadcasted_iota(jnp.int32, (tok, tok), 0) > lax.broadcasted_iota(jnp.int32, (tok, tok), 1)
+    ).astype(f32).astype(bf16)
+    earlier = jnp.dot(lower, (one0 + one1).astype(bf16), preferred_element_type=f32)
+    slot0 = jnp.sum(earlier * one0, axis=1, keepdims=True).astype(jnp.int32)
+    slot1 = jnp.sum(earlier * one1, axis=1, keepdims=True).astype(jnp.int32)
+    place0 = first * cap + slot0
+    place1 = second * cap + slot1
+    col = lax.broadcasted_iota(jnp.int32, (tok, chips * cap), 1)
+    hit0 = (col == place0).astype(f32)
+    hit1 = (col == place1).astype(f32)
+    gated = hit0 * gates[:, 0:1] + hit1 * gates[:, 1:2]
+    gate_hi = gated.astype(bf16)
+    gate_lo = (gated - gate_hi.astype(f32)).astype(bf16)
+    pick = (hit0 + hit1).T.astype(bf16)
+    normed = layer_norm(sources[...], enc_gain[...]).astype(bf16)
+    for h in range(2):
+        send[h] = jnp.dot(
+            pick, normed[:, h * half:(h + 1) * half], preferred_element_type=f32
+        ).astype(bf16)
+
+    pl.semaphore_wait(barrier, peers - 1 + (split - 1))
+
+    def slot_rows(i):
+        return pl.ds(pl.multiple_of(i * cap, 16), cap)
+
+    def dispatch(d):
+        to = lax.rem(me + d, peers)
+        return remote(
+            send.at[lax.rem(to, 2), slot_rows(lax.div(to, 2)), :],
+            rows.at[lax.rem(to, 2), slot_rows(me), :],
+            d_send.at[d], d_recv.at[me], {"expert": to},
+        )
+
+    def w_pair(i):
+        return remote(
+            weights[i].at[:, pl.ds(pl.multiple_of((1 - p) * half, 128), half)], wb.at[i, own_rows, :],
+            pair_send.at[i], pair_recv.at[i], {"expert": mate},
+        )
+
+    for i in range(4):
+        w_pair(i).start()
+    for d in range(1, peers):
+        dispatch(d).start()
+    self_rows = pltpu.make_async_copy(
+        send.at[p, slot_rows(chip), :], rows.at[p, slot_rows(me), :], loc_sem.at[6]
+    )
+    self_rows.start()
+
+    def blk(c, gg):
+        return wb.at[pl.ds(gg * mats, mats), pl.ds(pl.multiple_of(c * 2 * shard, 16), 2 * shard), :]
+
+    gw = g if split == 2 else 0
+
+    def w_up(zz):
+        c = zz * nx + x
+        return remote(blk(c, gw), blk(c, gw), up_send.at[zz], w_recv.at[c], dev_of(z + 1, x))
+
+    def w_dn(zz):
+        c = zz * nx + x
+        return remote(blk(c, gw), blk(c, gw), dn_send.at[zz], w_recv.at[c], dev_of(z - 1, x))
+
+    def w_x(zz):
+        c = zz * nx + x
+        return remote(blk(c, gw), blk(c, gw), x_send.at[zz], w_recv.at[c], dev_of(z, 1 - x))
+
+    def w_y(c):
+        return remote(blk(c, gw), blk(c, gw), y_send.at[c], y_recv.at[c], {"groups": 1 - g})
+
+    def w_got(c):
+        remote(blk(c, gw), blk(c, gw), x_send.at[0], w_recv.at[c], dev_of(z, x)).wait_recv()
+
+    for c in w_copies:
+        c.wait()
+    for i in range(4):
+        remote(
+            w_q.at[:, pl.ds(0, half)], wb.at[i, pl.ds(pl.multiple_of(mate * shard, 16), shard), :],
+            pair_send.at[i], pair_recv.at[i], {"expert": mate},
+        ).wait_recv()
+
+    can_up, can_dn = z < nz - 1, z > 0
+    pl.when(can_up)(lambda: w_up(z).start())
+    pl.when(can_dn)(lambda: w_dn(z).start())
+    if nx == 2:
+        w_x(z).start()
+
+    def relay(d):
+        @pl.when(z >= d)
+        def _():
+            w_got((z - d) * nx + x)
+            pl.when(can_up)(lambda: w_up(z - d).start())
+            if nx == 2:
+                w_x(z - d).start()
+            if split == 2:
+                w_y((z - d) * nx + x).start()
+
+        @pl.when(z + d < nz)
+        def _():
+            w_got((z + d) * nx + x)
+            pl.when(can_dn)(lambda: w_dn(z + d).start())
+            if nx == 2:
+                w_x(z + d).start()
+            if split == 2:
+                w_y((z + d) * nx + x).start()
+
+    per = tok // src_len.shape[0]
+    lane = lax.broadcasted_iota(jnp.int32, bias.shape[1:], 1)
+    limit = jnp.zeros(bias.shape[1:], jnp.int32)
+    for s in range(src_len.shape[0]):
+        limit = jnp.where(lax.div(lane, per) == s, src_len[s], limit)
+    bias[p] = jnp.where(lax.rem(lane, per) < limit, 0.0, -1e30).astype(f32)
+    tn[p] = layer_norm(targets[...], dec_gain[...]).astype(bf16)
+    tn_pair = remote(tn.at[p], tn.at[p], pair_send.at[4], pair_recv.at[4], {"expert": mate})
+    bias_pair = remote(bias.at[p], bias.at[p], pair_send.at[5], pair_recv.at[5], {"expert": mate})
+    tn_pair.start()
+    bias_pair.start()
+
+    self_rows.wait()
+    for d in range(1, peers):
+        frm = lax.rem(me + d, peers)
+        remote(
+            send.at[0, slot_rows(0), :], rows.at[p, slot_rows(frm), :], d_send.at[d], d_recv.at[frm], {"expert": mate}
+        ).wait_recv()
+    x_pair = remote(rows.at[p], rows.at[p], pair_send.at[6], pair_recv.at[6], {"expert": mate})
+    x_pair.start()
+    if nz > 1:
+        relay(1)
+    in_copy.wait()
+    remote(rows.at[1 - p], rows.at[1 - p], pair_send.at[6], pair_recv.at[6], {"expert": mate}).wait_recv()
+
+    ftile = 256
+
+    def up(i, _):
+        cols = pl.ds(pl.multiple_of(i * ftile, ftile), ftile)
+        acc = jnp.dot(rows[0], win[0:half, cols], preferred_element_type=f32)
+        acc += jnp.dot(rows[1], win[half:, cols], preferred_element_type=f32)
+        hid[:, cols] = jnp.maximum(acc, 0.0).astype(bf16)
+        return 0
+
+    lax.fori_loop(0, win.shape[1] // ftile, up, 0)
+    if nz > 2:
+        relay(2)
+    out_copy.wait()
+
+    def down(dst, base):
+        def body(i, _):
+            o = pl.multiple_of(i * ftile, ftile)
+            acc = jnp.dot(
+                hid[...], wout[:, pl.ds(pl.multiple_of(base + o, ftile), ftile)], preferred_element_type=f32
+            )
+            dst[:, pl.ds(o, ftile)] = acc.astype(bf16)
+            return 0
+
+        lax.fori_loop(0, half // ftile, body, 0)
+
+    down(away, (1 - p) * half)
+    y_pair = remote(away, inbox, pair_send.at[7], pair_recv.at[7], {"expert": mate})
+    y_pair.start()
+    down(own, p * half)
+    y_pair.wait_recv()
+    merged[...] = (own[...].astype(f32) + inbox[...].astype(f32)).astype(bf16)
+
+    def combine(d):
+        to = lax.rem(me + d, peers)
+        return remote(
+            merged.at[slot_rows(to), :], back.at[p, slot_rows(chip), :], c_send.at[d], c_recv.at[me], {"expert": to}
+        )
+
+    for d in range(1, peers):
+        combine(d).start()
+    self_back = pltpu.make_async_copy(
+        merged.at[slot_rows(me), :], back.at[p, slot_rows(chip), :], loc_sem.at[7]
+    )
+    self_back.start()
+    for d in range(3, nz):
+        relay(d)
+    if nx == 2:
+        for k in range(nz):
+            w_got(k * nx + 1 - x)
+            if split == 2:
+                w_y(k * nx + 1 - x).start()
+    self_back.wait()
+    for d in range(1, peers):
+        frm = lax.rem(me + d, peers)
+        remote(
+            merged.at[slot_rows(0), :], back.at[lax.rem(frm, 2), slot_rows(lax.div(frm, 2)), :],
+            c_send.at[d], c_recv.at[frm], {"expert": mate},
+        ).wait_recv()
+    for h in range(2):
+        cols = slice(h * half, (h + 1) * half)
+        moe = jnp.dot(gate_hi, back[h], preferred_element_type=f32)
+        moe += jnp.dot(gate_lo, back[h], preferred_element_type=f32)
+        mem[p, :, cols] = (sources[:, cols].astype(f32) + moe).astype(bf16)
+    m_pair = remote(mem.at[p], mem.at[p], pair_send.at[8], pair_recv.at[8], {"expert": mate})
+    m_pair.start()
+    memory[...] = mem[p]
+    remote(tn.at[1 - p], tn.at[1 - p], pair_send.at[4], pair_recv.at[4], {"expert": mate}).wait_recv()
+    remote(bias.at[1 - p], bias.at[1 - p], pair_send.at[5], pair_recv.at[5], {"expert": mate}).wait_recv()
+    if split == 2:
+        for c in range(1, chips):
+            cc = lax.rem(chip + c, chips)
+            remote(
+                blk(cc, 1 - g), blk(cc, 1 - g), y_send.at[cc], y_recv.at[cc], {"groups": 1 - g}
+            ).wait_recv()
+
+    qkv[0] = jnp.dot(
+        tn[...].reshape(2 * tok, width), wb[0], preferred_element_type=f32
+    ).astype(bf16)
+    remote(mem.at[1 - p], mem.at[1 - p], pair_send.at[8], pair_recv.at[8], {"expert": mate}).wait_recv()
+    both = mem[...].reshape(2 * tok, width)
+    for i in (1, 2):
+        qkv[i] = jnp.dot(both, wb[i], preferred_element_type=f32).astype(bf16)
+
+    r = lax.broadcasted_iota(jnp.int32, (2 * tok, tok), 0)
+    k = lax.broadcasted_iota(jnp.int32, (2 * tok, tok), 1)
+    same = lax.div(lax.rem(r, tok), per) == lax.div(k, per)
+    left = lax.broadcasted_iota(jnp.int32, (tok, 2 * DH), 1) < DH
+    for o in range(2):
+        keep = jnp.where(same, jnp.broadcast_to(bias[o, 0:1, :], (2 * tok, tok)), -1e30)
+        dead = keep < 0.0
+        for hp in range(half // (2 * DH)):
+            cols = slice(hp * 2 * DH, (hp + 1) * 2 * DH)
+            rws = slice(o * tok, (o + 1) * tok)
+            q2 = qkv[0, rws, cols]
+            zero = jnp.zeros_like(q2)
+            qs = jnp.concatenate((jnp.where(left, q2, zero), jnp.where(left, zero, q2)), axis=0)
+            sc = lax.dot_general(
+                qs, qkv[1, rws, cols], (((1,), (1,)), ((), ())), preferred_element_type=f32
+            ) * DH ** (-0.5)
+            sc = jnp.where(dead, -1e30, sc)
+            top = jnp.max(sc, axis=-1, keepdims=True)
+            raised = jnp.exp(sc - top)
+            wts = (raised / jnp.sum(raised, axis=-1, keepdims=True)).astype(bf16)
+            mixed = jnp.dot(wts, qkv[2, rws, cols], preferred_element_type=f32)
+            ctx[o, :, cols] = jnp.where(left, mixed[:tok], mixed[tok:]).astype(bf16)
+
+    def project(o):
+        return lax.dot_general(
+            ctx[o], wb[3], (((1,), (1,)), ((), ())), preferred_element_type=f32
+        )
+
+    give[...] = project(1 - p).astype(bf16)
+    o_pair = remote(give, take, pair_send.at[9], pair_recv.at[9], {"expert": mate})
+    o_pair.start()
+    mine = project(p)
+    pos = lax.broadcasted_iota(jnp.int32, (tok, width), 0)
+    per_t = tok // tgt_len.shape[0]
+    tlimit = jnp.zeros((tok, width), jnp.int32)
+    for s in range(tgt_len.shape[0]):
+        tlimit = jnp.where(lax.div(pos, per_t) == s, tgt_len[s], tlimit)
+    live = lax.rem(pos, per_t) < tlimit
+    o_pair.wait_recv()
+    total = targets[...].astype(f32) + (mine + take[...].astype(f32))
+    decoded[...] = jnp.where(live, total, 0.0).astype(bf16)
+
+    for i in range(4):
+        w_pair(i).wait_send()
+    for c in (tn_pair, bias_pair, x_pair, y_pair, m_pair, o_pair):
+        c.wait_send()
+    for d in range(1, peers):
+        dispatch(d).wait_send()
+        combine(d).wait_send()
+    pl.when(can_up)(lambda: w_up(z).wait_send())
+    pl.when(can_dn)(lambda: w_dn(z).wait_send())
+    if nx == 2:
+        w_x(z).wait_send()
+    for d in range(1, nz):
+        @pl.when(z >= d)
+        def _():
+            pl.when(can_up)(lambda: w_up(z - d).wait_send())
+            if nx == 2:
+                w_x(z - d).wait_send()
+            if split == 2:
+                w_y((z - d) * nx + x).wait_send()
+
+        @pl.when(z + d < nz)
+        def _():
+            pl.when(can_dn)(lambda: w_dn(z + d).wait_send())
+            if nx == 2:
+                w_x(z + d).wait_send()
+            if split == 2:
+                w_y((z + d) * nx + x).wait_send()
+    if nx == 2 and split == 2:
+        for k in range(nz):
+            w_y(k * nx + 1 - x).wait_send()
+
+
+def fused(
+    sources, enc_gain, route_ids, route_gates, w_in, w_out, targets, dec_gain,
+    src_lengths, tgt_lengths, w_query, w_key, w_value, w_attn,
+):
+    tok, width = sources.shape
+    peers = lax.axis_size("expert")
+    chips = peers // 2
+    half = width // 2
+    capacity = 2 * ((5 * tok + 4 * chips - 1) // (4 * chips))
+    cap = (capacity + 15) // 16 * 16
+    hidden = w_in.shape[2]
+    bf16 = jnp.bfloat16
+    vm, sm, anym = (
+        pl.BlockSpec(memory_space=pltpu.VMEM),
+        pl.BlockSpec(memory_space=pltpu.SMEM),
+        pl.BlockSpec(memory_space=pl.ANY),
+    )
+    dma = pltpu.SemaphoreType.DMA
+    return pl.pallas_call(
+        fused_kernel,
+        out_shape=(jax.ShapeDtypeStruct((tok, width), bf16),) * 2,
+        in_specs=[sm, sm, vm, vm, vm, vm, anym, anym, vm, vm, anym, anym, anym, anym],
+        out_specs=(vm, vm),
+        scratch_shapes=[
+            pltpu.VMEM((width, hidden), bf16),
+            pltpu.VMEM((hidden, width), bf16),
+            pltpu.VMEM((4, width, half), bf16),
+            pltpu.VMEM((2, chips * cap, half), bf16),
+            pltpu.VMEM((2, peers * cap, half), bf16),
+            pltpu.VMEM((peers * cap, hidden), bf16),
+            pltpu.VMEM((peers * cap, half), bf16),
+            pltpu.VMEM((peers * cap, half), bf16),
+            pltpu.VMEM((peers * cap, half), bf16),
+            pltpu.VMEM((peers * cap, half), bf16),
+            pltpu.VMEM((2, chips * cap, half), bf16),
+            pltpu.VMEM((2, tok, width), bf16),
+            pltpu.VMEM((2, tok, width), bf16),
+            pltpu.VMEM((2, 8, tok), jnp.float32),
+            pltpu.VMEM((3, 2 * tok, half), bf16),
+            pltpu.VMEM((2, tok, half), bf16),
+            pltpu.VMEM((tok, width), bf16),
+            pltpu.VMEM((tok, width), bf16),
+            dma((8,)), dma((10,)), dma((10,)),
+            dma((peers,)), dma((peers,)), dma((peers,)), dma((peers,)),
+            dma((chips,)), dma((chips,)), dma((chips,)), dma((chips,)), dma((chips,)), dma((chips,)),
+        ],
+        compiler_params=pltpu.CompilerParams(
+            collective_id=0, has_side_effects=True, vmem_limit_bytes=56 * 1024 * 1024
+        ),
+    )(
+        src_lengths, tgt_lengths, sources, enc_gain.reshape(1, -1), route_ids, route_gates,
+        w_in, w_out, targets, dec_gain.reshape(1, -1), w_query, w_key, w_value, w_attn,
+    )
+
+
 def solution(mesh):
     placed = (
         P(("groups", "expert"), None),
@@ -138,8 +546,9 @@
         P("expert", "head"),
         P("expert", "head"),
     )
+    body = fused if mesh.shape["head"] == 1 else shards
     return jax.shard_map(
-        shards,
+        body,
         mesh=mesh,
         in_specs=placed,
         out_specs=(P(("groups", "expert"), None), P(("groups", "expert"), "head")),

time: 202 us -> 89.6 us (0.44)
  the two profiles are of different devices: /device:TPU:0 before, /device:TPU:25 now
where the time goes in v1:
time: 89.6 us; the launch traced here: 89.4 us
  Pallas kernels  82.6 us (92%)
  local copies, waits for them, and re-layouts  6.17 us (7%)
    pallas_call x1, Pallas kernels, fused(): pl.pallas_call(fused_kernel, out_shape=(jax.ShapeDtypeStruct((tok, width)...  82.6 us
    unnamed x4, local copies, waits for them, and re-layouts  6.17 us

profile of v1, /device:TPU:25, one launch (start us, length us, event | category | flops | bytes accessed | tf_op | source)
XLA Modules:
  0.0 89.4 jit_solution(2748678558510094624)
XLA Ops:
  0.6 1.4 %copy.16.ids = s32[128,2]{1,0:T(8,128)} copy(s32[128,2]{0,1:T(2,128)} %param.16) | data formatting | bytes 2048 | tf_op args[2]
  2.0 1.4 %copy.17.gates = f32[128,2]{1,0:T(8,128)} copy(f32[128,2]{0,1:T(2,128)} %param.17) | data formatting | bytes 2048 | tf_op args[3]
  3.5 82.6 %shard_map.149 = (bf16[128,1024]{1,0:T(8,128)(2,1)}, bf16[128,1024]{1,0:T(8,128)(2,1)}) custom-call(s32[2]{0:T(128)} %src_len.1, s32[2]{0:T(128)} %tgt_len.1, bf16[128,1024]{1,0:T(8,128)(2,1)} %sources.1, f32[1,1024]{1,0:T(1,128)} %bitcast.2, s32[128,2]{1,0:T(8,128)} %copy.16.ids, f32[128,2]{1,0:T(8,128)} %copy.17.gates, bf16[1,1024,2048]{2,1,0:T(8,128)(2,1)} %w_in.1, ...), custom_call_target="tpu_custom_call" | custom-call | tf_op jit(solution)/shard_map/pallas_call | solution.py:495
  86.1 1.7 %copy.20 = bf16[128,1024]{1,0:T(8,128)(2,1)} copy(bf16[128,1024]{1,0:T(8,128)(2,1)} %get-tuple-element.4) | data formatting | bytes 524288
  87.7 1.7 %copy.21 = bf16[128,1024]{1,0:T(8,128)(2,1)} copy(bf16[128,1024]{1,0:T(8,128)(2,1)} %get-tuple-element.5) | data formatting | bytes 524288
